TPU v7x, 512 devices: a whole 4x8x8 slice. The times are simulated.
512 devices in a mesh: patch: 16 (over y_lo, x), dir: 32 (over y_hi, z, core).
Axes of the slice: x: 4, y: 8 (y_hi: 2, y_lo: 4; y = y_hi * 4 + y_lo), z: 8, core: 2. Of those that a mesh axis runs over, the one named last changes fastest.
Arguments:
- fine_out: bfloat16 [96, 128, 2, 4, 512], P('patch', 'dir'), may hold values from -6 to 6
- interp: bfloat16 [512, 2048], replicated, may hold values from -0.25 to 0.25
- child_phase: float32 [4, 2048], replicated, may hold values from -3.140625 to 3.140625
- fine_ops: float32 [40, 2, 512], replicated, may hold values from -1.2 to 1.2
- parent_ops: float32 [40, 2, 2048], P(None, None, 'dir'), may hold values from -0.6 to 0.6
- fine_src: int32 [96, 128, 32], P('patch'), may hold values from 0 to 12287, as said below
- fine_op: int32 [96, 128, 32], P('patch'), may hold values from 0 to 40, as said below
- parent_src: int32 [48, 64, 32], P('patch'), may hold values from 0 to 3071, as said below
- parent_op: int32 [48, 64, 32], P('patch'), may hold values from 0 to 40, as said below
Outputs:
- fine_in: float32 [96, 128, 2, 4, 512], P('patch', 'dir')
Inputs may be any that keep to these rules, and one draw needn't show every extreme that they name: `fine_src`: A slot with op id 40 is padding and names the box itself. Every other slot names a distinct box at most 3 rows and 3 columns away, not adjacent to the box, whose parent is adjacent to or equal to the box's parent; its op id is the index of the offset (dr, dc), in order of dr then dc over -3..3, among the offsets with max(|dr|, |dc|) > 1. `fine_op`: as for fine_src. `parent_src`: as for fine_src, on the parent grid. `parent_op`: as for fine_op, on the parent grid.
All inputs are finite; a program needn't handle non-finite values.
Results may differ from a plain program's by a relative error of at most 0.0022.
Values may be sent and summed in bfloat16 or wider, within the bound.
A program may use at most 128 MiB of HBM per device.

v0:
```python
import jax
import jax.numpy as jnp
from jax import lax
from jax.experimental import pallas as pl
from jax.experimental.pallas import tpu as pltpu
from jax.sharding import PartitionSpec as P

MESH = pl.DeviceIdType.MESH
ZN = 8
OFFSETS = [(a, b) for a in range(-3, 4) for b in range(-3, 4) if max(abs(a), abs(b)) > 1]
F32, BF16 = jnp.float32, jnp.bfloat16


def flip(v):
    turned = pltpu.roll(v, 4, 0)
    top = lax.broadcasted_iota(jnp.int32, v.shape, 0) < 4
    return jnp.where(top, -turned, turned)


def row_of(ref, r, lanes):
    return ref[pl.ds(r, 1), lanes]


def aggregate(blk, first_slot, count, interp, cosine, sine, parents, places):
    def chunk(n, carry):
        lanes = pl.ds(pl.multiple_of(n * 256, 256), 256)
        rows = blk[pl.ds(first_slot * 192, count * 192), :]
        spread = jnp.dot(rows, interp[:, lanes], preferred_element_type=F32)
        cos_at = [row_of(cosine, k, lanes) for k in range(4)]
        sin_at = [row_of(sine, k, lanes) for k in range(4)]
        for which, (row, col) in enumerate(places):
            for pr in range(3):
                for pc in range(2):
                    first = second = None
                    for k in range(4):
                        start = which * 192 + ((2 * pr + k // 2) * 4 + 2 * pc + k % 2) * 8
                        part = spread[start : start + 8]
                        a, b = cos_at[k] * part, sin_at[k] * part
                        first = a if first is None else first + a
                        second = b if second is None else second + b
                    value = first + flip(second)
                    parents[row + pr, col + pc, :, lanes] = value.astype(BF16).astype(F32)
        return carry

    lax.fori_loop(0, interp.shape[1] // 256, chunk, 0, unroll=2)


def widen(blk, slot, window, row0, rows, row_at, col0, cols, col_at):
    for r in range(rows):
        for c in range(0, cols, 2):
            start = slot * 192 + ((row0 + r) * 4 + col0 + c) * 8
            pair = blk[start : start + 16, :].astype(F32)
            window[row_at + r, col_at + c] = pair[:8]
            window[row_at + r, col_at + c + 1] = pair[8:]


def near_field(window, ops, present, near, core, late):
    def is_late(col):
        return col < 2 if core == 0 else col >= 6

    def one(step, carry):
        pair, lane = step // 4, lax.rem(step, 4)
        lanes = pl.ds(pl.multiple_of(lane * 128, 128), 128)
        first, second = {}, {}
        for op, (dr, dc) in enumerate(OFFSETS):
            used = [
                (kr, c)
                for kr in range(2)
                for c in range(4)
                if -2 - kr <= dr <= 3 - kr and -2 - c % 2 <= dc <= 3 - c % 2 and is_late(2 + c + dc) == late
            ]
            if not used:
                continue
            cos_part = ops[op, pl.ds(0, 1), lanes]
            sin_part = ops[op, pl.ds(1, 1), lanes]
            for t in used:
                kr, c = t
                source = window[2 * pair + 2 + kr + dr, 2 + c + dc, :, lanes]
                source = source * present[(2 * pair + kr) * 4 + c, op]
                a, b = cos_part * source, sin_part * source
                first[t] = first[t] + a if t in first else a
                second[t] = second[t] + b if t in second else b
        for t in first:
            value = first[t] + flip(second[t])
            box = (2 * pair + t[0]) * 4 + t[1]
            near[box, :, lanes] = near[box, :, lanes] + value if late else value
        return carry

    lax.fori_loop(0, 12, one, 0)


def far_sums(parents, cos_ops, sin_ops, present, lanes, core, odd, late):
    def is_late(col):
        return col < 2 if core == 0 else col >= 4

    first, second = {}, {}
    for op, (dr, dc) in enumerate(OFFSETS):
        used = [
            (pr, pc)
            for pr in range(3)
            for pc in range(2)
            if -2 - (odd + pr) % 2 <= dr <= 3 - (odd + pr) % 2
            and -2 - pc <= dc <= 3 - pc
            and is_late(2 + pc + dc) == late
        ]
        if not used:
            continue
        cos_part = row_of(cos_ops, op, lanes)
        sin_part = row_of(sin_ops, op, lanes)
        for t in used:
            pr, pc = t
            source = parents[3 + pr + dr, 2 + pc + dc, :, lanes]
            source = source * present[24 + pr * 2 + pc, op]
            a, b = cos_part * source, sin_part * source
            first[t] = first[t] + a if t in first else a
            second[t] = second[t] + b if t in second else b
    return {t: first[t] + flip(second[t]) for t in first}


def far_early(parents, cos_ops, sin_ops, present, parent_in, core, odd):
    def one(n, carry):
        lanes = pl.ds(pl.multiple_of(n * 256, 256), 256)
        sums = far_sums(parents, cos_ops, sin_ops, present, lanes, core, odd, False)
        for (pr, pc), value in sums.items():
            parent_in[pr * 2 + pc, :, lanes] = value
        return carry

    lax.fori_loop(0, parent_in.shape[-1] // 256, one, 0)


def far_late(parents, cos_ops, sin_ops, present, parent_in, cosine, sine, child, core, odd):
    def one(n, carry):
        lanes = pl.ds(pl.multiple_of(n * 256, 256), 256)
        sums = far_sums(parents, cos_ops, sin_ops, present, lanes, core, odd, True)
        for pr in range(3):
            for pc in range(2):
                value = parent_in[pr * 2 + pc, :, lanes] + sums[(pr, pc)]
                value = value.astype(BF16).astype(F32)
                turned = flip(value)
                for kr in range(2):
                    both = [
                        row_of(cosine, 2 * kr + kc, lanes) * value - row_of(sine, 2 * kr + kc, lanes) * turned
                        for kc in range(2)
                    ]
                    box = (2 * pr + kr) * 4 + 2 * pc
                    child[box * 8 : box * 8 + 16, lanes] = jnp.concatenate(both, axis=0).astype(BF16)
        return carry

    lax.fori_loop(0, parent_in.shape[-1] // 256, one, 0)


def kernel(
    x_hbm, ops_hbm, interp_hbm, phase_hbm, fine_ops_hbm, fine_list_hbm, par_list_hbm, out,
    blk, opsg, x_raw, ops_raw, interp, phase, fine_ops, fine_list, par_list, on_vec, on,
    parents, window, near, parent_in, child, cosine, sine, cos_ops, sin_ops,
    ssem, rsem, lsem, ysem, zs, zr, es, er,
):
    np_, nd = lax.axis_size("patch"), lax.axis_size("dir")
    p, d = lax.axis_index("patch"), lax.axis_index("dir")
    core, z, y = lax.rem(d, 2), lax.rem(d // 2, ZN), d // (2 * ZN)
    odd = lax.rem(p, 2)
    up, down = lax.rem(p + 1, np_), lax.rem(p + np_ - 1, np_)
    other = d + 1 - 2 * core
    outer = lax.rem(d - 1 + 2 * core + nd, nd)
    far = lax.rem(d + 2 * ZN, nd)
    has_up, has_down = p < np_ - 1, p > 0
    has_outer = jnp.logical_and(d > 0, d < nd - 1)
    z_peer = [(p, y * 2 * ZN + lax.rem(z + k, ZN) * 2 + core) for k in range(ZN)]
    barrier = pltpu.get_barrier_semaphore()

    def greet(peer):
        pl.semaphore_signal(barrier, inc=1, device_id=peer, device_id_type=MESH)

    for peer in [(p, other), (p, far)] + z_peer[1:]:
        greet(peer)
    pl.when(has_up)(lambda: greet((up, d)))
    pl.when(has_down)(lambda: greet((down, d)))
    pl.when(has_outer)(lambda: greet((p, outer)))

    pairs = [
        (x_hbm, x_raw), (ops_hbm, ops_raw), (phase_hbm, phase), (interp_hbm, interp),
        (fine_list_hbm, fine_list), (par_list_hbm, par_list), (fine_ops_hbm, fine_ops),
    ]
    loads = [pltpu.make_async_copy(a, b, lsem.at[i]) for i, (a, b) in enumerate(pairs)]
    for load in loads:
        load.start()
    loads[0].wait()
    for r in range(6):
        for c in range(0, 4, 2):
            parts = [x_raw[r, c + i // 2, i % 2].astype(F32) for i in range(4)]
            blk[(r * 4 + c) * 8 : (r * 4 + c) * 8 + 16, :] = jnp.concatenate(parts, axis=0).astype(BF16)
    loads[1].wait()
    opsg[core, z, y] = jnp.concatenate([ops_raw[:, 0, :], ops_raw[:, 1, :]], axis=1)

    one = lambda flag: flag.astype(jnp.int32)
    pl.semaphore_wait(barrier, 2 + ZN - 1 + one(has_up) + one(has_down) + one(has_outer))

    def at(slot, count=1):
        return blk.at[pl.ds(slot * 192, count * 192)]

    def send(src, dst, s, r, peer):
        return pltpu.make_async_remote_copy(
            src_ref=src, dst_ref=dst, send_sem=s, recv_sem=r, device_id=peer, device_id_type=MESH
        )

    def block(src, dst, peer):
        return send(at(src), at(dst), ssem.at[dst - 1], rsem.at[dst - 1], peer)

    to_other, to_outer = block(0, 1, (p, other)), block(0, 2, (p, outer))
    to_up, to_down = block(0, 3, (up, d)), block(0, 4, (down, d))
    up_other, down_other = block(3, 5, (p, other)), block(4, 6, (p, other))
    outer_up, outer_down = block(2, 7, (up, d)), block(2, 8, (down, d))
    to_far = send(opsg.at[core, z, y], opsg.at[core, z, y], ysem.at[0], ysem.at[1], (p, far))

    to_far.start()
    pl.when(has_outer)(lambda: to_outer.start())
    pl.when(has_up)(lambda: to_up.start())
    pl.when(has_down)(lambda: to_down.start())
    to_other.start()

    def z_send(k):
        ref = opsg.at[core, z]
        return send(ref, ref, zs.at[k], zr.at[k], z_peer[k])

    def z_arrival(k):
        ref = opsg.at[core, lax.rem(z - k + ZN, ZN)]
        return send(ref, ref, zs.at[k], zr.at[k], z_peer[k])

    def pass_on(k):
        ref = opsg.at[core, lax.rem(z - k + ZN, ZN)]
        return send(ref, ref, es.at[k], er.at[k], (p, other))

    def clear(slots):
        for slot in slots:
            blk[slot * 192 : (slot + 1) * 192, :] = jnp.zeros((192, 512), BF16)

    pl.when(jnp.logical_not(has_down))(lambda: clear((3, 5, 7)))
    pl.when(jnp.logical_not(has_up))(lambda: clear((4, 6, 8)))
    pl.when(jnp.logical_and(jnp.logical_not(has_outer), has_down))(lambda: clear((7,)))
    pl.when(jnp.logical_and(jnp.logical_not(has_outer), has_up))(lambda: clear((8,)))
    pl.when(jnp.logical_not(has_outer))(lambda: clear((2,)))

    loads[2].wait()
    cosine[...] = jnp.cos(phase[...])
    sine[...] = jnp.sin(phase[...])
    loads[4].wait()
    loads[5].wait()
    kind = lax.broadcasted_iota(jnp.int32, (32, 128), 1)
    for r in range(6):
        lists = fine_list[r]
        for c in range(4):
            mine = jnp.sum(jnp.where(kind == 4 * d + c, lists, 0), axis=1, keepdims=True)
            on_vec[r * 4 + c : r * 4 + c + 1, :] = jnp.sum(jnp.where(mine == kind, 1.0, 0.0), axis=0, keepdims=True)
    kind64 = lax.broadcasted_iota(jnp.int32, (32, 64), 1)
    for r in range(3):
        lists = par_list[r]
        for c in range(2):
            mine = jnp.sum(jnp.where(kind64 == 2 * d + c, lists, 0), axis=1, keepdims=True)
            row = 24 + r * 2 + c
            on_vec[row : row + 1, :] = jnp.sum(jnp.where(mine == kind, 1.0, 0.0), axis=0, keepdims=True)
    to_smem = pltpu.make_async_copy(on_vec, on, lsem.at[7])
    to_smem.start()

    other_col, outer_col = 4 - 4 * core, 4 * core
    loads[3].wait()
    to_other.wait_recv()
    aggregate(blk, 0, 2, interp, cosine, sine, parents, [(3, 2), (3, other_col)])

    to_far.wait()
    for k in (1, 7, 2, 6, 3, 5, 4):
        z_send(k).start()
    pass_on(0).start()

    @pl.when(has_outer)
    def _():
        to_outer.wait_recv()
        pl.when(has_up)(lambda: outer_up.start())
        pl.when(has_down)(lambda: outer_down.start())

    @pl.when(has_down)
    def _():
        to_up.wait_recv()
        up_other.start()

    @pl.when(has_up)
    def _():
        to_down.wait_recv()
        down_other.start()

    aggregate(blk, 2, 3, interp, cosine, sine, parents, [(3, outer_col), (0, 2), (6, 2)])
    for k in (1, 7, 2, 6, 3, 5, 4):
        z_arrival(k).wait_recv()
        pass_on(k).start()
    pl.when(has_down)(lambda: up_other.wait_recv())
    pl.when(has_up)(lambda: down_other.wait_recv())
    aggregate(blk, 5, 2, interp, cosine, sine, parents, [(0, other_col), (6, other_col)])

    def widen_strips(slots, row0, rows, row_at, col0, cols, col_at):
        for slot, a, b, c in zip(slots, row0, rows, row_at):
            widen(blk, slot, window, a, b, c, col0, cols, col_at)

    widen_strips((0, 3, 4), (0, 4, 0), (6, 2, 2), (2, 0, 8), 0, 4, 2)
    pl.when(core == 0)(lambda: widen_strips((1, 5, 6), (0, 4, 0), (6, 2, 2), (2, 0, 8), 0, 2, 6))
    pl.when(core == 1)(lambda: widen_strips((1, 5, 6), (0, 4, 0), (6, 2, 2), (2, 0, 8), 2, 2, 0))
    to_smem.wait()
    loads[6].wait()
    for which in range(2):
        pl.when(core == which)(lambda which=which: near_field(window, fine_ops, on, near, which, False))

    for k in range(ZN):
        pass_on(k).wait_recv()

    def gather_ops(chunk, carry):
        lanes = pl.ds(pl.multiple_of(chunk * 128, 128), 128)
        even, uneven = (opsg[i, lax.rem(chunk, ZN), chunk // ZN] for i in range(2))
        low = lax.broadcasted_iota(jnp.int32, even.shape, 1) < 64
        cos_ops[:, lanes] = jnp.where(low, even, pltpu.roll(uneven, 64, 1))
        sin_ops[:, lanes] = jnp.where(low, pltpu.roll(even, 64, 1), uneven)
        return carry

    lax.fori_loop(0, 2 * ZN, gather_ops, 0)
    variants = [(a, b) for a in range(2) for b in range(2)]
    for a, b in variants:
        pl.when(jnp.logical_and(core == a, odd == b))(
            lambda a=a, b=b: far_early(parents, cos_ops, sin_ops, on, parent_in, a, b)
        )

    pl.when(jnp.logical_and(has_outer, has_down))(lambda: outer_up.wait_recv())
    pl.when(jnp.logical_and(has_outer, has_up))(lambda: outer_down.wait_recv())
    aggregate(blk, 7, 2, interp, cosine, sine, parents, [(0, outer_col), (6, outer_col)])
    for a, b in variants:
        pl.when(jnp.logical_and(core == a, odd == b))(
            lambda a=a, b=b: far_late(parents, cos_ops, sin_ops, on, parent_in, cosine, sine, child, a, b)
        )
    pl.when(core == 0)(lambda: widen_strips((2, 7, 8), (0, 4, 0), (6, 2, 2), (2, 0, 8), 2, 2, 0))
    pl.when(core == 1)(lambda: widen_strips((2, 7, 8), (0, 4, 0), (6, 2, 2), (2, 0, 8), 0, 2, 6))
    for which in range(2):
        pl.when(core == which)(lambda which=which: near_field(window, fine_ops, on, near, which, True))
    back = lax.dot_general(child[...], interp[...], (((1,), (1,)), ((), ())), preferred_element_type=F32)
    scale = interp.shape[0] / interp.shape[1]
    for r in range(6):
        for c in range(4):
            box = r * 4 + c
            total = near[box] + back[box * 8 : box * 8 + 8] * scale
            out[r, c, 0] = total[:4]
            out[r, c, 1] = total[4:]

    to_other.wait_send()
    pl.when(has_outer)(lambda: to_outer.wait_send())
    pl.when(has_up)(lambda: to_up.wait_send())
    pl.when(has_down)(lambda: to_down.wait_send())
    pl.when(has_down)(lambda: up_other.wait_send())
    pl.when(has_up)(lambda: down_other.wait_send())
    pl.when(jnp.logical_and(has_outer, has_up))(lambda: outer_up.wait_send())
    pl.when(jnp.logical_and(has_outer, has_down))(lambda: outer_down.wait_send())
    for k in range(1, ZN):
        z_send(k).wait_send()
    for k in range(ZN):
        pass_on(k).wait_send()


def per_device(
    fine_out, interp, child_phase, fine_ops, parent_ops, fine_src, fine_op, parent_src, parent_op
):
    dp = interp.shape[1]
    kinds = fine_ops.shape[0]
    dma = pltpu.SemaphoreType.DMA
    hbm = pl.BlockSpec(memory_space=pl.ANY)
    vmem = pltpu.VMEM
    fine_list, par_list = (jnp.transpose(v, (0, 2, 1)) for v in (fine_op, parent_op))
    return pl.pallas_call(
        kernel,
        out_shape=jax.ShapeDtypeStruct(fine_out.shape, F32),
        in_specs=[hbm] * 7,
        out_specs=pl.BlockSpec(memory_space=pltpu.VMEM),
        scratch_shapes=[
            vmem((9 * 192, 512), BF16),
            vmem((2, ZN, 2, kinds, 128), F32),
            vmem(fine_out.shape, BF16),
            vmem(parent_ops.shape, F32),
            vmem(interp.shape, BF16),
            vmem((4, dp), F32),
            vmem(fine_ops.shape, F32),
            vmem(fine_list.shape, jnp.int32),
            vmem(par_list.shape, jnp.int32),
            vmem((32, 128), F32),
            pltpu.SMEM((32, 128), F32),
            vmem((9, 6, 8, dp), F32),
            vmem((10, 8, 8, 512), F32),
            vmem((24, 8, 512), F32),
            vmem((6, 8, dp), F32),
            vmem((192, dp), BF16),
            vmem((4, dp), F32),
            vmem((4, dp), F32),
            vmem((kinds, dp), F32),
            vmem((kinds, dp), F32),
            dma((8,)), dma((8,)), dma((8,)), dma((2,)), dma((ZN,)), dma((ZN,)), dma((ZN,)), dma((ZN,)),
        ],
        compiler_params=pltpu.CompilerParams(
            collective_id=0, has_side_effects=True, vmem_limit_bytes=56 * 1024 * 1024
        ),
        name="fmm",
    )(fine_out, parent_ops, interp, child_phase, fine_ops, fine_list, par_list)


def solution(mesh):
    in_specs = (
        P("patch", "dir", None, None, None),
        P(),
        P(),
        P(),
        P(None, None, "dir"),
        P("patch", None, None),
        P("patch", None, None),
        P("patch", None, None),
        P("patch", None, None),
    )
    out_specs = P("patch", "dir", None, None, None)
    return jax.shard_map(
        per_device, mesh=mesh, in_specs=in_specs, out_specs=out_specs, check_vma=False
    )
```

profile of v0, /device:TPU:56, one launch (start us, length us, event | category | flops | bytes accessed | tf_op | source)
XLA Modules:
  0.0 41.2 jit_solution(1370383513898305458)
XLA Ops:
  0.0 39.4 %fmm.1 = f32[6,4,2,4,512]{4,3,2,1,0:T(4,128)} custom-call(bf16[6,4,2,4,512]{4,3,2,1,0:T(4,128)(2,1)} %x_hbm.1, f32[40,2,64]{2,1,0:T(2,128)} %ops_hbm.1, bf16[512,2048]{1,0:T(8,128)(2,1)} %interp_hbm.1, f32[4,2048]{1,0:T(4,128)} %phase_hbm.1, f32[40,2,512]{2,1,0:T(2,128)} %fine_ops_hbm.1, s32[6,32,128]{2,1,0:T(8,128)} %bitcast.2, s32[3,32,64]{2,1,0:T(8,128)} %bitcast.3), custom_call_target="tpu_custom_call" | custom-call | tf_op jit(solution)/shard_map/fmm/pallas_call | solution.py:371
  39.4 1.8 %copy.9 = f32[6,4,2,4,512]{4,3,2,1,0:T(4,128)} copy(f32[6,4,2,4,512]{4,3,2,1,0:T(4,128)} %fmm.1) | data formatting | bytes 786432
where the time goes:
time: 41.3 us; the launch traced here: 41.2 us
  Pallas kernels  39.4 us (95%)
  local copies, waits for them, and re-layouts  1.78 us (4%)
    pallas_call x1, Pallas kernels, per_device(): pl.pallas_call(kernel, out_shape=jax.ShapeDtypeStruct(fine_out.shape, F32...  39.4 us
    unnamed x1, local copies, waits for them, and re-layouts  1.78 us

commit v1 on v0

v1 whole, which is shorter than its diff:
```python
import jax
import jax.numpy as jnp
from jax import lax
from jax.experimental import pallas as pl
from jax.experimental.pallas import tpu as pltpu
from jax.sharding import PartitionSpec as P

MESH = pl.DeviceIdType.MESH
ZN = 8
OFFSETS = [(a, b) for a in range(-3, 4) for b in range(-3, 4) if max(abs(a), abs(b)) > 1]
F32, BF16 = jnp.float32, jnp.bfloat16


def flip(v):
    turned = pltpu.roll(v, 4, 0)
    top = lax.broadcasted_iota(jnp.int32, v.shape, 0) < 4
    return jnp.where(top, -turned, turned)


def row_of(ref, r, lanes):
    return ref[pl.ds(r, 1), lanes]


def aggregate(x, interp, cosine, sine, packed, parents):
    rows = x.reshape(192, 512)

    def chunk(n, carry):
        lanes = pl.ds(pl.multiple_of(n * 256, 256), 256)
        spread = jnp.dot(rows, interp[:, lanes], preferred_element_type=F32)
        cos_at = [row_of(cosine, k, lanes) for k in range(4)]
        sin_at = [row_of(sine, k, lanes) for k in range(4)]
        for pr in range(3):
            pair = []
            for pc in range(2):
                first = second = None
                for k in range(4):
                    start = ((2 * pr + k // 2) * 4 + 2 * pc + k % 2) * 8
                    part = spread[start : start + 8]
                    a, b = cos_at[k] * part, sin_at[k] * part
                    first = a if first is None else first + a
                    second = b if second is None else second + b
                pair.append(first + flip(second))
            rounded = jnp.concatenate(pair, axis=0).astype(BF16)
            packed[pr * 16 : pr * 16 + 16, lanes] = rounded
            wide = rounded.astype(F32)
            parents[3 + pr, 2, :, lanes] = wide[:8]
            parents[3 + pr, 3, :, lanes] = wide[8:]
        return carry

    lax.fori_loop(0, interp.shape[1] // 256, chunk, 0, unroll=2)


def place(packed, slot, parents, row, col):
    for pr in range(3):
        wide = packed[slot * 48 + pr * 16 : slot * 48 + pr * 16 + 16, :].astype(F32)
        parents[row + pr, col] = wide[:8]
        parents[row + pr, col + 1] = wide[8:]


def widen(strip, window, rows, col_at):
    for r in rows:
        pair = strip(r).astype(F32)
        window[r, col_at] = pair[:8]
        window[r, col_at + 1] = pair[8:]


def near_field(window, ops, present, near, core, late, start, stop):
    def is_late(col):
        return col < 2 if core == 0 else col >= 6

    def one(step, carry):
        pair, lane = step // 4, lax.rem(step, 4)
        lanes = pl.ds(pl.multiple_of(lane * 128, 128), 128)
        first, second = {}, {}
        for op, (dr, dc) in enumerate(OFFSETS):
            used = [
                (kr, c)
                for kr in range(2)
                for c in range(4)
                if -2 - kr <= dr <= 3 - kr and -2 - c % 2 <= dc <= 3 - c % 2 and is_late(2 + c + dc) == late
            ]
            if not used:
                continue
            cos_part = ops[op, pl.ds(0, 1), lanes]
            sin_part = ops[op, pl.ds(1, 1), lanes]
            for t in used:
                kr, c = t
                source = window[2 * pair + 2 + kr + dr, 2 + c + dc, :, lanes]
                source = source * present[(2 * pair + kr) * 4 + c, op]
                a, b = cos_part * source, sin_part * source
                first[t] = first[t] + a if t in first else a
                second[t] = second[t] + b if t in second else b
        for t in first:
            value = first[t] + flip(second[t])
            box = (2 * pair + t[0]) * 4 + t[1]
            near[box, :, lanes] = near[box, :, lanes] + value if late else value
        return carry

    lax.fori_loop(start, stop, one, 0)


def far_sums(parents, cos_ops, sin_ops, present, lanes, core, odd, late):
    def is_late(col):
        return col < 2 if core == 0 else col >= 4

    first, second = {}, {}
    for op, (dr, dc) in enumerate(OFFSETS):
        used = [
            (pr, pc)
            for pr in range(3)
            for pc in range(2)
            if -2 - (odd + pr) % 2 <= dr <= 3 - (odd + pr) % 2
            and -2 - pc <= dc <= 3 - pc
            and is_late(2 + pc + dc) == late
        ]
        if not used:
            continue
        cos_part = row_of(cos_ops, op, lanes)
        sin_part = row_of(sin_ops, op, lanes)
        for t in used:
            pr, pc = t
            source = parents[3 + pr + dr, 2 + pc + dc, :, lanes]
            source = source * present[24 + pr * 2 + pc, op]
            a, b = cos_part * source, sin_part * source
            first[t] = first[t] + a if t in first else a
            second[t] = second[t] + b if t in second else b
    return {t: first[t] + flip(second[t]) for t in first}


def far_early(parents, cos_ops, sin_ops, present, parent_in, core, odd):
    def one(n, carry):
        lanes = pl.ds(pl.multiple_of(n * 256, 256), 256)
        sums = far_sums(parents, cos_ops, sin_ops, present, lanes, core, odd, False)
        for (pr, pc), value in sums.items():
            parent_in[pr * 2 + pc, :, lanes] = value
        return carry

    lax.fori_loop(0, parent_in.shape[-1] // 256, one, 0)


def far_late(parents, cos_ops, sin_ops, present, parent_in, cosine, sine, child, core, odd):
    def one(n, carry):
        lanes = pl.ds(pl.multiple_of(n * 256, 256), 256)
        sums = far_sums(parents, cos_ops, sin_ops, present, lanes, core, odd, True)
        for pr in range(3):
            for pc in range(2):
                value = parent_in[pr * 2 + pc, :, lanes] + sums[(pr, pc)]
                value = value.astype(BF16).astype(F32)
                turned = flip(value)
                for kr in range(2):
                    both = [
                        row_of(cosine, 2 * kr + kc, lanes) * value - row_of(sine, 2 * kr + kc, lanes) * turned
                        for kc in range(2)
                    ]
                    box = (2 * pr + kr) * 4 + 2 * pc
                    child[box * 8 : box * 8 + 16, lanes] = jnp.concatenate(both, axis=0).astype(BF16)
        return carry

    lax.fori_loop(0, parent_in.shape[-1] // 256, one, 0)


def kernel(
    x_hbm, ops_hbm, interp_hbm, phase_hbm, fine_ops_hbm, fine_list_hbm, par_list_hbm, out,
    packed, own, oth, outr, opsg, x_raw, ops_raw, interp, phase, fine_ops, fine_list, par_list, on_vec, on,
    parents, window, near, parent_in, child, cosine, sine, cos_ops, sin_ops,
    ssem, rsem, fs, fr, lsem, ysem, zs, zr, es, er,
):
    np_, nd = lax.axis_size("patch"), lax.axis_size("dir")
    p, d = lax.axis_index("patch"), lax.axis_index("dir")
    core, z, y = lax.rem(d, 2), lax.rem(d // 2, ZN), d // (2 * ZN)
    odd = lax.rem(p, 2)
    up, down = lax.rem(p + 1, np_), lax.rem(p + np_ - 1, np_)
    other = d + 1 - 2 * core
    outer = lax.rem(d - 1 + 2 * core + nd, nd)
    far = lax.rem(d + 2 * ZN, nd)
    has_up, has_down = p < np_ - 1, p > 0
    has_outer = jnp.logical_and(d > 0, d < nd - 1)
    both_up, both_down = jnp.logical_and(has_outer, has_up), jnp.logical_and(has_outer, has_down)
    z_peer = [(p, y * 2 * ZN + lax.rem(z + k, ZN) * 2 + core) for k in range(ZN)]
    barrier = pltpu.get_barrier_semaphore()

    def greet(peer):
        pl.semaphore_signal(barrier, inc=1, device_id=peer, device_id_type=MESH)

    for peer in [(p, other), (p, far)] + z_peer[1:]:
        greet(peer)
    pl.when(has_up)(lambda: greet((up, d)))
    pl.when(has_down)(lambda: greet((down, d)))
    pl.when(has_outer)(lambda: greet((p, outer)))

    pairs = [
        (x_hbm, x_raw), (phase_hbm, phase), (interp_hbm, interp), (ops_hbm, ops_raw),
        (fine_list_hbm, fine_list), (par_list_hbm, par_list), (fine_ops_hbm, fine_ops),
    ]
    loads = [pltpu.make_async_copy(a, b, lsem.at[i]) for i, (a, b) in enumerate(pairs)]
    for load in loads:
        load.start()
    loads[1].wait()
    cosine[...] = jnp.cos(phase[...])
    sine[...] = jnp.sin(phase[...])
    loads[0].wait()
    for r in range(6):
        for c in range(0, 4, 2):
            parts = [x_raw[r, c + i // 2, i % 2].astype(F32) for i in range(4)]
            own[r + 2, c // 2] = jnp.concatenate(parts, axis=0).astype(BF16)
    loads[3].wait()
    opsg[core, z, y] = jnp.concatenate([ops_raw[:, 0, :], ops_raw[:, 1, :]], axis=1).astype(BF16)
    loads[2].wait()
    aggregate(own[2:8], interp, cosine, sine, packed, parents)

    one = lambda flag: flag.astype(jnp.int32)
    pl.semaphore_wait(barrier, 2 + ZN - 1 + one(has_up) + one(has_down) + one(has_outer))

    def send(src, dst, s, r, peer):
        return pltpu.make_async_remote_copy(
            src_ref=src, dst_ref=dst, send_sem=s, recv_sem=r, device_id=peer, device_id_type=MESH
        )

    def block(src, dst, peer):
        a, b = packed.at[pl.ds(src * 48, 48)], packed.at[pl.ds(dst * 48, 48)]
        return send(a, b, ssem.at[dst - 1], rsem.at[dst - 1], peer)

    def strip(slot, src, dst, peer):
        return send(src, dst, fs.at[slot - 1], fr.at[slot - 1], peer)

    low, mid, high = pl.ds(0, 2), pl.ds(2, 6), pl.ds(8, 2)
    first_rows, last_rows = pl.ds(2, 2), pl.ds(6, 2)
    routes = {
        1: (True, True, (p, other)),
        2: (has_outer, has_outer, (p, outer)),
        3: (has_up, has_down, (up, d)),
        4: (has_down, has_up, (down, d)),
        5: (has_down, has_down, (p, other)),
        6: (has_up, has_up, (p, other)),
        7: (both_up, both_down, (up, d)),
        8: (both_down, both_up, (down, d)),
    }
    source = {1: 0, 2: 0, 3: 0, 4: 0, 5: 3, 6: 4, 7: 2, 8: 2}
    blocks = {s: block(source[s], s, routes[s][2]) for s in routes}
    strips = {
        1: strip(1, own.at[mid, 1 - core], oth.at[mid], (p, other)),
        2: strip(2, own.at[mid, core], outr.at[mid], (p, outer)),
        3: strip(3, own.at[last_rows], own.at[low], (up, d)),
        4: strip(4, own.at[first_rows], own.at[high], (down, d)),
        5: strip(5, own.at[low, 1 - core], oth.at[low], (p, other)),
        6: strip(6, own.at[high, 1 - core], oth.at[high], (p, other)),
        7: strip(7, outr.at[last_rows], outr.at[low], (up, d)),
        8: strip(8, outr.at[first_rows], outr.at[high], (down, d)),
    }

    def when(flag, act):
        act() if flag is True else pl.when(flag)(act)

    def start(kind, slot):
        when(routes[slot][0], lambda: kind[slot].start())

    def arrive(kind, slot):
        when(routes[slot][1], lambda: kind[slot].wait_recv())

    own_ops, far_ops = opsg.at[core, z, y], opsg.at[core, z, 1 - y]
    to_far = send(own_ops, own_ops, ysem.at[0], ysem.at[1], (p, far))
    near_first = (1, 7, 2, 6, 3, 5, 4)

    def z_send(k, half):
        ref = opsg.at[core, z, y if half == 0 else 1 - y]
        return send(ref, ref, zs.at[half, k], zr.at[half, k], z_peer[k])

    def z_arrival(k, half):
        ref = opsg.at[core, lax.rem(z - k + ZN, ZN), y if half == 0 else 1 - y]
        return send(ref, ref, zs.at[half, k], zr.at[half, k], z_peer[k])

    def pass_on(k):
        ref = opsg.at[core, lax.rem(z - k + ZN, ZN)]
        return send(ref, ref, es.at[k], er.at[k], (p, other))

    to_far.start()
    for slot in (2, 3, 4, 1):
        start(strips, slot)
    for slot in (2, 3, 4):
        start(blocks, slot)
    for k in near_first:
        z_send(k, 0).start()
    start(blocks, 1)

    other_col, outer_col = 4 - 4 * core, 4 * core
    spots = {1: (3, other_col), 2: (3, outer_col), 3: (0, 2), 4: (6, 2), 5: (0, other_col), 6: (6, other_col),
             7: (0, outer_col), 8: (6, outer_col)}

    def settle(slot):
        row, col = spots[slot]
        arrive(blocks, slot)
        when(routes[slot][1], lambda: place(packed, slot, parents, row, col))
        if routes[slot][1] is not True:

            @pl.when(jnp.logical_not(routes[slot][1]))
            def _():
                for pr in range(3):
                    for pc in range(2):
                        parents[row + pr, col + pc] = jnp.zeros(parents.shape[2:], F32)

    def blank(ref, flag):
        @pl.when(jnp.logical_not(flag))
        def _():
            ref[...] = jnp.zeros(ref.shape, BF16)

    blank(own.at[low], has_down)
    blank(own.at[high], has_up)
    blank(oth.at[low], has_down)
    blank(oth.at[high], has_up)
    blank(outr.at[mid], has_outer)
    blank(outr.at[low], both_down)
    blank(outr.at[high], both_up)

    loads[4].wait()
    loads[5].wait()
    kind = lax.broadcasted_iota(jnp.int32, (32, 128), 1)
    for r in range(6):
        lists = fine_list[r]
        for c in range(4):
            mine = jnp.sum(jnp.where(kind == 4 * d + c, lists, 0), axis=1, keepdims=True)
            on_vec[r * 4 + c : r * 4 + c + 1, :] = jnp.sum(jnp.where(mine == kind, 1.0, 0.0), axis=0, keepdims=True)
    kind64 = lax.broadcasted_iota(jnp.int32, (32, 64), 1)
    for r in range(3):
        lists = par_list[r]
        for c in range(2):
            mine = jnp.sum(jnp.where(kind64 == 2 * d + c, lists, 0), axis=1, keepdims=True)
            row = 24 + r * 2 + c
            on_vec[row : row + 1, :] = jnp.sum(jnp.where(mine == kind, 1.0, 0.0), axis=0, keepdims=True)
    to_smem = pltpu.make_async_copy(on_vec, on, lsem.at[7])
    to_smem.start()

    arrive(strips, 3)
    start(strips, 5)
    arrive(strips, 4)
    start(strips, 6)
    to_far.wait()
    for k in near_first:
        z_send(k, 1).start()
    pass_on(0).start()
    arrive(strips, 1)
    for c in range(2):
        widen(lambda r, c=c: own[r, c], window, range(10), 2 + 2 * c)
    for slot in (5, 6):
        arrive(strips, slot)
    widen(lambda r: oth[r], window, range(10), 6 - 6 * core)
    settle(1)
    to_smem.wait()
    loads[6].wait()

    def near_part(late, begin, end):
        for which in range(2):
            pl.when(core == which)(
                lambda which=which: near_field(window, fine_ops, on, near, which, late, begin, end)
            )

    crossing = jnp.logical_or(d == 2 * ZN - 1, d == 2 * ZN)

    def relay(flag):
        @pl.when(jnp.logical_and(has_outer, flag))
        def _():
            strips[2].wait_recv()
            blocks[2].wait_recv()
            for slot in (7, 8):
                start(strips, slot)
                start(blocks, slot)

    relay(jnp.logical_not(crossing))
    near_part(False, 0, 4)
    relay(crossing)
    arrive(blocks, 3)
    start(blocks, 5)
    arrive(blocks, 4)
    start(blocks, 6)
    for k in near_first:
        z_arrival(k, 0).wait_recv()
        z_arrival(k, 1).wait_recv()
        pass_on(k).start()
    near_part(False, 4, 12)

    def place_only(slot):
        row, col = spots[slot]
        when(routes[slot][1], lambda: place(packed, slot, parents, row, col))
        if routes[slot][1] is not True:

            @pl.when(jnp.logical_not(routes[slot][1]))
            def _():
                for pr in range(3):
                    for pc in range(2):
                        parents[row + pr, col + pc] = jnp.zeros(parents.shape[2:], F32)

    for slot in (3, 4, 2):
        place_only(slot)
    for slot in (5, 6):
        settle(slot)
    for k in range(ZN):
        pass_on(k).wait_recv()

    def gather_ops(chunk, carry):
        lanes = pl.ds(pl.multiple_of(chunk * 128, 128), 128)
        even, uneven = (opsg[i, lax.rem(chunk, ZN), chunk // ZN].astype(F32) for i in range(2))
        left = lax.broadcasted_iota(jnp.int32, even.shape, 1) < 64
        cos_ops[:, lanes] = jnp.where(left, even, pltpu.roll(uneven, 64, 1))
        sin_ops[:, lanes] = jnp.where(left, pltpu.roll(even, 64, 1), uneven)
        return carry

    lax.fori_loop(0, 2 * ZN, gather_ops, 0)
    variants = [(a, b) for a in range(2) for b in range(2)]
    for a, b in variants:
        pl.when(jnp.logical_and(core == a, odd == b))(
            lambda a=a, b=b: far_early(parents, cos_ops, sin_ops, on, parent_in, a, b)
        )
    for slot in (7, 8):
        arrive(strips, slot)
    widen(lambda r: outr[r], window, range(10), 6 * core)
    near_part(True, 0, 12)
    for slot in (7, 8):
        settle(slot)
    for a, b in variants:
        pl.when(jnp.logical_and(core == a, odd == b))(
            lambda a=a, b=b: far_late(parents, cos_ops, sin_ops, on, parent_in, cosine, sine, child, a, b)
        )
    back = lax.dot_general(child[...], interp[...], (((1,), (1,)), ((), ())), preferred_element_type=F32)
    scale = interp.shape[0] / interp.shape[1]
    for r in range(6):
        for c in range(4):
            box = r * 4 + c
            total = near[box] + back[box * 8 : box * 8 + 8] * scale
            out[r, c, 0] = total[:4]
            out[r, c, 1] = total[4:]

    to_far_done = [z_send(k, half) for k in range(1, ZN) for half in range(2)] + [pass_on(k) for k in range(ZN)]
    for copy in to_far_done:
        copy.wait_send()
    for kind_of in (strips, blocks):
        for slot in routes:
            when(routes[slot][0], lambda kind_of=kind_of, slot=slot: kind_of[slot].wait_send())


def per_device(
    fine_out, interp, child_phase, fine_ops, parent_ops, fine_src, fine_op, parent_src, parent_op
):
    dp = interp.shape[1]
    kinds = fine_ops.shape[0]
    dma = pltpu.SemaphoreType.DMA
    hbm = pl.BlockSpec(memory_space=pl.ANY)
    vmem = pltpu.VMEM
    fine_list, par_list = (jnp.transpose(v, (0, 2, 1)) for v in (fine_op, parent_op))
    return pl.pallas_call(
        kernel,
        out_shape=jax.ShapeDtypeStruct(fine_out.shape, F32),
        in_specs=[hbm] * 7,
        out_specs=pl.BlockSpec(memory_space=pltpu.VMEM),
        scratch_shapes=[
            vmem((9 * 48, dp), BF16),
            vmem((10, 2, 16, 512), BF16),
            vmem((10, 16, 512), BF16),
            vmem((10, 16, 512), BF16),
            vmem((2, ZN, 2, kinds, 128), BF16),
            vmem(fine_out.shape, BF16),
            vmem(parent_ops.shape, F32),
            vmem(interp.shape, BF16),
            vmem((4, dp), F32),
            vmem(fine_ops.shape, F32),
            vmem(fine_list.shape, jnp.int32),
            vmem(par_list.shape, jnp.int32),
            vmem((32, 128), F32),
            pltpu.SMEM((32, 128), F32),
            vmem((9, 6, 8, dp), F32),
            vmem((10, 8, 8, 512), F32),
            vmem((24, 8, 512), F32),
            vmem((6, 8, dp), F32),
            vmem((192, dp), BF16),
            vmem((4, dp), F32),
            vmem((4, dp), F32),
            vmem((kinds, dp), F32),
            vmem((kinds, dp), F32),
            dma((8,)), dma((8,)), dma((8,)), dma((8,)), dma((8,)), dma((2,)),
            dma((2, ZN)), dma((2, ZN)), dma((ZN,)), dma((ZN,)),
        ],
        compiler_params=pltpu.CompilerParams(
            collective_id=0, has_side_effects=True, vmem_limit_bytes=56 * 1024 * 1024
        ),
        name="fmm",
    )(fine_out, parent_ops, interp, child_phase, fine_ops, fine_list, par_list)


def solution(mesh):
    in_specs = (
        P("patch", "dir", None, None, None),
        P(),
        P(),
        P(),
        P(None, None, "dir"),
        P("patch", None, None),
        P("patch", None, None),
        P("patch", None, None),
        P("patch", None, None),
    )
    out_specs = P("patch", "dir", None, None, None)
    return jax.shard_map(
        per_device, mesh=mesh, in_specs=in_specs, out_specs=out_specs, check_vma=False
    )
```

time: 41.3 us -> 39.6 us (0.959); the launches traced: 41.2 us -> 38.9 us
  Pallas kernels: 39.4 us -> 37.1 us
    pallas_call x1, Pallas kernels: 39.4 us -> 37.1 us  [per_device(): pl.pallas_call(kernel, out_shape=jax.ShapeDtypeStruct(fine_out.shape, F32...]
where the time goes in v1:
time: 39.6 us; the launch traced here: 38.9 us
  Pallas kernels  37.1 us (94%)
  local copies, waits for them, and re-layouts  1.78 us (4%)
    pallas_call x1, Pallas kernels, per_device(): pl.pallas_call(kernel, out_shape=jax.ShapeDtypeStruct(fine_out.shape, F32...  37.1 us
    unnamed x1, local copies, waits for them, and re-layouts  1.78 us

profile of v1, /device:TPU:56, one launch (start us, length us, event | category | flops | bytes accessed | tf_op | source)
XLA Modules:
  0.0 38.9 jit_solution(17262270255323957727)
XLA Ops:
  0.0 37.1 %fmm.1 = f32[6,4,2,4,512]{4,3,2,1,0:T(4,128)} custom-call(bf16[6,4,2,4,512]{4,3,2,1,0:T(4,128)(2,1)} %x_hbm.1, f32[40,2,64]{2,1,0:T(2,128)} %ops_hbm.1, bf16[512,2048]{1,0:T(8,128)(2,1)} %interp_hbm.1, f32[4,2048]{1,0:T(4,128)} %phase_hbm.1, f32[40,2,512]{2,1,0:T(2,128)} %fine_ops_hbm.1, s32[6,32,128]{2,1,0:T(8,128)} %bitcast.2, s32[3,32,64]{2,1,0:T(8,128)} %bitcast.3), custom_call_target="tpu_custom_call" | custom-call | tf_op jit(solution)/shard_map/fmm/pallas_call | solution.py:448
  37.1 1.8 %copy.9 = f32[6,4,2,4,512]{4,3,2,1,0:T(4,128)} copy(f32[6,4,2,4,512]{4,3,2,1,0:T(4,128)} %fmm.1) | data formatting | bytes 786432

commit v2 on v1

--- a/solution.py
+++ b/solution.py
@@ -7,6 +7,8 @@
 
 MESH = pl.DeviceIdType.MESH
 ZN = 8
+PIECE = 512
+OWN, LEFT, RIGHT = (2, 3, 4, 5), (0, 1), (6, 7)
 OFFSETS = [(a, b) for a in range(-3, 4) for b in range(-3, 4) if max(abs(a), abs(b)) > 1]
 F32, BF16 = jnp.float32, jnp.bfloat16
 
@@ -21,11 +23,10 @@
     return ref[pl.ds(r, 1), lanes]
 
 
-def aggregate(x, interp, cosine, sine, packed, parents):
-    rows = x.reshape(192, 512)
-
-    def chunk(n, carry):
-        lanes = pl.ds(pl.multiple_of(n * 256, 256), 256)
+def aggregate(own, interp, cosine, sine, packed, parents, q):
+    rows = own[2:8].reshape(192, 512)
+    for half in range(2):
+        lanes = pl.ds(pl.multiple_of(q * PIECE + half * 256, 256), 256)
         spread = jnp.dot(rows, interp[:, lanes], preferred_element_type=F32)
         cos_at = [row_of(cosine, k, lanes) for k in range(4)]
         sin_at = [row_of(sine, k, lanes) for k in range(4)]
@@ -41,20 +42,18 @@
                     second = b if second is None else second + b
                 pair.append(first + flip(second))
             rounded = jnp.concatenate(pair, axis=0).astype(BF16)
-            packed[pr * 16 : pr * 16 + 16, lanes] = rounded
+            packed[q, pr * 16 : pr * 16 + 16, half * 256 : half * 256 + 256] = rounded
             wide = rounded.astype(F32)
             parents[3 + pr, 2, :, lanes] = wide[:8]
             parents[3 + pr, 3, :, lanes] = wide[8:]
-        return carry
-
-    lax.fori_loop(0, interp.shape[1] // 256, chunk, 0, unroll=2)
-
-
-def place(packed, slot, parents, row, col):
+
+
+def place(packed, slot, parents, row, col, q):
+    lanes = pl.ds(pl.multiple_of(q * PIECE, PIECE), PIECE)
     for pr in range(3):
-        wide = packed[slot * 48 + pr * 16 : slot * 48 + pr * 16 + 16, :].astype(F32)
-        parents[row + pr, col] = wide[:8]
-        parents[row + pr, col + 1] = wide[8:]
+        wide = packed[q, slot * 48 + pr * 16 : slot * 48 + pr * 16 + 16, :].astype(F32)
+        parents[row + pr, col, :, lanes] = wide[:8]
+        parents[row + pr, col + 1, :, lanes] = wide[8:]
 
 
 def widen(strip, window, rows, col_at):
@@ -64,10 +63,7 @@
         window[r, col_at + 1] = pair[8:]
 
 
-def near_field(window, ops, present, near, core, late, start, stop):
-    def is_late(col):
-        return col < 2 if core == 0 else col >= 6
-
+def near_field(window, ops, present, near, columns, start, stop):
     def one(step, carry):
         pair, lane = step // 4, lax.rem(step, 4)
         lanes = pl.ds(pl.multiple_of(lane * 128, 128), 128)
@@ -77,7 +73,7 @@
                 (kr, c)
                 for kr in range(2)
                 for c in range(4)
-                if -2 - kr <= dr <= 3 - kr and -2 - c % 2 <= dc <= 3 - c % 2 and is_late(2 + c + dc) == late
+                if -2 - kr <= dr <= 3 - kr and -2 - c % 2 <= dc <= 3 - c % 2 and 2 + c + dc in columns
             ]
             if not used:
                 continue
@@ -93,7 +89,7 @@
         for t in first:
             value = first[t] + flip(second[t])
             box = (2 * pair + t[0]) * 4 + t[1]
-            near[box, :, lanes] = near[box, :, lanes] + value if late else value
+            near[box, :, lanes] = value if columns is OWN else near[box, :, lanes] + value
         return carry
 
     lax.fori_loop(start, stop, one, 0)
@@ -127,7 +123,7 @@
     return {t: first[t] + flip(second[t]) for t in first}
 
 
-def far_early(parents, cos_ops, sin_ops, present, parent_in, core, odd):
+def far_early(parents, cos_ops, sin_ops, present, parent_in, core, odd, q):
     def one(n, carry):
         lanes = pl.ds(pl.multiple_of(n * 256, 256), 256)
         sums = far_sums(parents, cos_ops, sin_ops, present, lanes, core, odd, False)
@@ -135,10 +131,10 @@
             parent_in[pr * 2 + pc, :, lanes] = value
         return carry
 
-    lax.fori_loop(0, parent_in.shape[-1] // 256, one, 0)
-
-
-def far_late(parents, cos_ops, sin_ops, present, parent_in, cosine, sine, child, core, odd):
+    lax.fori_loop(q * (PIECE // 256), (q + 1) * (PIECE // 256), one, 0)
+
+
+def far_late(parents, cos_ops, sin_ops, present, parent_in, cosine, sine, child, core, odd, q):
     def one(n, carry):
         lanes = pl.ds(pl.multiple_of(n * 256, 256), 256)
         sums = far_sums(parents, cos_ops, sin_ops, present, lanes, core, odd, True)
@@ -156,14 +152,14 @@
                     child[box * 8 : box * 8 + 16, lanes] = jnp.concatenate(both, axis=0).astype(BF16)
         return carry
 
-    lax.fori_loop(0, parent_in.shape[-1] // 256, one, 0)
+    lax.fori_loop(q * (PIECE // 256), (q + 1) * (PIECE // 256), one, 0)
 
 
 def kernel(
     x_hbm, ops_hbm, interp_hbm, phase_hbm, fine_ops_hbm, fine_list_hbm, par_list_hbm, out,
     packed, own, oth, outr, opsg, x_raw, ops_raw, interp, phase, fine_ops, fine_list, par_list, on_vec, on,
     parents, window, near, parent_in, child, cosine, sine, cos_ops, sin_ops,
-    ssem, rsem, fs, fr, lsem, ysem, zs, zr, es, er,
+    ssem, rsem, fs, fr, lsem, isem, ysem, zs, zr, es, er,
 ):
     np_, nd = lax.axis_size("patch"), lax.axis_size("dir")
     p, d = lax.axis_index("patch"), lax.axis_index("dir")
@@ -188,12 +184,22 @@
     pl.when(has_down)(lambda: greet((down, d)))
     pl.when(has_outer)(lambda: greet((p, outer)))
 
+    pieces = interp.shape[1] // PIECE
     pairs = [
-        (x_hbm, x_raw), (phase_hbm, phase), (interp_hbm, interp), (ops_hbm, ops_raw),
+        (x_hbm, x_raw), (phase_hbm, phase), (ops_hbm, ops_raw),
         (fine_list_hbm, fine_list), (par_list_hbm, par_list), (fine_ops_hbm, fine_ops),
     ]
     loads = [pltpu.make_async_copy(a, b, lsem.at[i]) for i, (a, b) in enumerate(pairs)]
-    for load in loads:
+
+    def interp_load(q):
+        lanes = pl.ds(pl.multiple_of(q * PIECE, PIECE), PIECE)
+        return pltpu.make_async_copy(interp_hbm.at[:, lanes], interp.at[:, lanes], isem.at[q])
+
+    for load in loads[:2]:
+        load.start()
+    for q in range(pieces):
+        interp_load(q).start()
+    for load in loads[2:]:
         load.start()
     loads[1].wait()
     cosine[...] = jnp.cos(phase[...])
@@ -203,10 +209,8 @@
         for c in range(0, 4, 2):
             parts = [x_raw[r, c + i // 2, i % 2].astype(F32) for i in range(4)]
             own[r + 2, c // 2] = jnp.concatenate(parts, axis=0).astype(BF16)
-    loads[3].wait()
-    opsg[core, z, y] = jnp.concatenate([ops_raw[:, 0, :], ops_raw[:, 1, :]], axis=1).astype(BF16)
     loads[2].wait()
-    aggregate(own[2:8], interp, cosine, sine, packed, parents)
+    opsg[core, z, y] = jnp.concatenate([ops_raw[:, 0, :], ops_raw[:, 1, :]], axis=1).astype(opsg.dtype)
 
     one = lambda flag: flag.astype(jnp.int32)
     pl.semaphore_wait(barrier, 2 + ZN - 1 + one(has_up) + one(has_down) + one(has_outer))
@@ -215,10 +219,6 @@
         return pltpu.make_async_remote_copy(
             src_ref=src, dst_ref=dst, send_sem=s, recv_sem=r, device_id=peer, device_id_type=MESH
         )
-
-    def block(src, dst, peer):
-        a, b = packed.at[pl.ds(src * 48, 48)], packed.at[pl.ds(dst * 48, 48)]
-        return send(a, b, ssem.at[dst - 1], rsem.at[dst - 1], peer)
 
     def strip(slot, src, dst, peer):
         return send(src, dst, fs.at[slot - 1], fr.at[slot - 1], peer)
@@ -236,7 +236,25 @@
         8: (both_down, both_up, (down, d)),
     }
     source = {1: 0, 2: 0, 3: 0, 4: 0, 5: 3, 6: 4, 7: 2, 8: 2}
-    blocks = {s: block(source[s], s, routes[s][2]) for s in routes}
+
+    even = odd == 0
+    not_even = odd == 1
+    short_send = {3: not_even, 4: even, 5: even, 6: not_even, 7: not_even, 8: even}
+    short_recv = {3: even, 4: not_even, 5: even, 6: not_even, 7: even, 8: not_even}
+
+    def block(slot, q, short=False, src=None, peer=None):
+        first, count = (16 if slot % 2 else 0, 32) if short else (0, 48)
+        src = source[slot] if src is None else src
+        a, b = (packed.at[q, pl.ds(i * 48 + first, count)] for i in (src, slot))
+        return send(a, b, ssem.at[q, slot - 1], rsem.at[q, slot - 1], routes[slot][2] if peer is None else peer)
+
+    def each_size(slot, flag, short, act):
+        if slot < 3:
+            when(flag, lambda: act(False))
+        else:
+            pl.when(jnp.logical_and(flag, short[slot]))(lambda: act(True))
+            pl.when(jnp.logical_and(flag, jnp.logical_not(short[slot])))(lambda: act(False))
+
     strips = {
         1: strip(1, own.at[mid, 1 - core], oth.at[mid], (p, other)),
         2: strip(2, own.at[mid, core], outr.at[mid], (p, outer)),
@@ -251,13 +269,35 @@
     def when(flag, act):
         act() if flag is True else pl.when(flag)(act)
 
-    def start(kind, slot):
-        when(routes[slot][0], lambda: kind[slot].start())
-
-    def arrive(kind, slot):
-        when(routes[slot][1], lambda: kind[slot].wait_recv())
-
-    own_ops, far_ops = opsg.at[core, z, y], opsg.at[core, z, 1 - y]
+    def start(slot):
+        when(routes[slot][0], lambda: strips[slot].start())
+
+    def arrive(slot):
+        when(routes[slot][1], lambda: strips[slot].wait_recv())
+
+    def start_block(slot, q):
+        each_size(slot, sends[slot], short_send, lambda short: block(slot, q, short).start())
+
+    def arrive_block(slot, q):
+        each_size(slot, routes[slot][1], short_recv, lambda short: block(slot, q, short).wait_recv())
+
+    def sent_block(slot, q):
+        each_size(slot, sends[slot], short_send, lambda short: block(slot, q, short).wait_send())
+
+    def across(slot, q):
+        return block(slot, q, True, slot - 4, (p, outer))
+
+    crossing = jnp.logical_or(d == 2 * ZN - 1, d == 2 * ZN)
+    direct = jnp.logical_and(has_outer, jnp.logical_not(crossing))
+    run = 4
+    edge_low = jnp.logical_and(lax.rem(p, run) == 0, has_down)
+    edge_high = jnp.logical_and(lax.rem(p, run) == run - 1, has_up)
+    hand_on = {7: jnp.logical_and(direct, edge_low), 8: jnp.logical_and(direct, edge_high)}
+    sends = {s: routes[s][0] for s in routes}
+    sends[7] = jnp.logical_and(both_up, jnp.logical_not(hand_on[8]))
+    sends[8] = jnp.logical_and(both_down, jnp.logical_not(hand_on[7]))
+
+    own_ops = opsg.at[core, z, y]
     to_far = send(own_ops, own_ops, ysem.at[0], ysem.at[1], (p, far))
     near_first = (1, 7, 2, 6, 3, 5, 4)
 
@@ -269,34 +309,41 @@
         ref = opsg.at[core, lax.rem(z - k + ZN, ZN), y if half == 0 else 1 - y]
         return send(ref, ref, zs.at[half, k], zr.at[half, k], z_peer[k])
 
-    def pass_on(k):
-        ref = opsg.at[core, lax.rem(z - k + ZN, ZN)]
-        return send(ref, ref, es.at[k], er.at[k], (p, other))
-
+    def pass_on(k, half):
+        ref = opsg.at[core, lax.rem(z - k + ZN, ZN), y if half == 0 else 1 - y]
+        return send(ref, ref, es.at[half, k], er.at[half, k], (p, other))
+
+    for slot in (2, 3, 4, 1):
+        start(slot)
     to_far.start()
-    for slot in (2, 3, 4, 1):
-        start(strips, slot)
-    for slot in (2, 3, 4):
-        start(blocks, slot)
     for k in near_first:
         z_send(k, 0).start()
-    start(blocks, 1)
+
+    def following(q, carry):
+        interp_load(q).wait()
+        aggregate(own, interp, cosine, sine, packed, parents, q)
+        for slot in (2, 3, 4, 1):
+            start_block(slot, q)
+        return carry
+
+    lax.fori_loop(0, pieces, following, 0)
 
     other_col, outer_col = 4 - 4 * core, 4 * core
     spots = {1: (3, other_col), 2: (3, outer_col), 3: (0, 2), 4: (6, 2), 5: (0, other_col), 6: (6, other_col),
              7: (0, outer_col), 8: (6, outer_col)}
 
-    def settle(slot):
+    def settle(slot, q):
         row, col = spots[slot]
-        arrive(blocks, slot)
-        when(routes[slot][1], lambda: place(packed, slot, parents, row, col))
-        if routes[slot][1] is not True:
-
-            @pl.when(jnp.logical_not(routes[slot][1]))
-            def _():
-                for pr in range(3):
-                    for pc in range(2):
-                        parents[row + pr, col + pc] = jnp.zeros(parents.shape[2:], F32)
+        when(routes[slot][1], lambda: place(packed, slot, parents, row, col, q))
+
+    for slot in range(2, 9):
+
+        @pl.when(jnp.logical_not(routes[slot][1]))
+        def _(slot=slot):
+            row, col = spots[slot]
+            for pr in range(3):
+                for pc in range(2):
+                    parents[row + pr, col + pc] = jnp.zeros(parents.shape[2:], F32)
 
     def blank(ref, flag):
         @pl.when(jnp.logical_not(flag))
@@ -311,8 +358,8 @@
     blank(outr.at[low], both_down)
     blank(outr.at[high], both_up)
 
+    loads[3].wait()
     loads[4].wait()
-    loads[5].wait()
     kind = lax.broadcasted_iota(jnp.int32, (32, 128), 1)
     for r in range(6):
         lists = fine_list[r]
@@ -326,74 +373,68 @@
             mine = jnp.sum(jnp.where(kind64 == 2 * d + c, lists, 0), axis=1, keepdims=True)
             row = 24 + r * 2 + c
             on_vec[row : row + 1, :] = jnp.sum(jnp.where(mine == kind, 1.0, 0.0), axis=0, keepdims=True)
-    to_smem = pltpu.make_async_copy(on_vec, on, lsem.at[7])
+    to_smem = pltpu.make_async_copy(on_vec, on, lsem.at[6])
     to_smem.start()
 
-    arrive(strips, 3)
-    start(strips, 5)
-    arrive(strips, 4)
-    start(strips, 6)
+    def relay(q):
+        block(2, q).wait_recv()
+        for slot in (7, 8):
+            start_block(slot, q)
+
+    def relay_strips():
+        strips[2].wait_recv()
+        for slot in (7, 8):
+            start(slot)
+
+    def forward(q):
+        for slot in (3, 4):
+            arrive_block(slot, q)
+            start_block(slot + 2, q)
+            pl.when(hand_on[slot + 4])(lambda slot=slot: across(slot + 4, q).start())
+        pl.when(direct)(lambda: relay(q))
+
+    def near_side(columns_of):
+        for which in range(2):
+            pl.when(core == which)(
+                lambda which=which: near_field(window, fine_ops, on, near, columns_of[which], 0, 12)
+            )
+
+    def relay_crossing(*qs):
+        @pl.when(crossing)
+        def _():
+            for q in qs:
+                relay(q)
+
+    def collect(half):
+        for k in near_first:
+            z_arrival(k, half).wait_recv()
+            pass_on(k, half).start()
+
+    for slot in (3, 4):
+        arrive(slot)
+        start(slot + 2)
+    for c in range(2):
+        widen(lambda r, c=c: own[r, c], window, range(10), 2 + 2 * c)
+    to_smem.wait()
+    loads[5].wait()
+    near_field(window, fine_ops, on, near, OWN, 0, 4)
     to_far.wait()
     for k in near_first:
         z_send(k, 1).start()
-    pass_on(0).start()
-    arrive(strips, 1)
-    for c in range(2):
-        widen(lambda r, c=c: own[r, c], window, range(10), 2 + 2 * c)
-    for slot in (5, 6):
-        arrive(strips, slot)
+    for half in range(2):
+        pass_on(0, half).start()
+    forward(0)
+    near_field(window, fine_ops, on, near, OWN, 4, 8)
+    forward(1)
+    pl.when(direct)(relay_strips)
+    near_field(window, fine_ops, on, near, OWN, 8, 12)
+    collect(0)
+    forward(2)
+    for slot in (1, 5, 6):
+        arrive(slot)
     widen(lambda r: oth[r], window, range(10), 6 - 6 * core)
-    settle(1)
-    to_smem.wait()
-    loads[6].wait()
-
-    def near_part(late, begin, end):
-        for which in range(2):
-            pl.when(core == which)(
-                lambda which=which: near_field(window, fine_ops, on, near, which, late, begin, end)
-            )
-
-    crossing = jnp.logical_or(d == 2 * ZN - 1, d == 2 * ZN)
-
-    def relay(flag):
-        @pl.when(jnp.logical_and(has_outer, flag))
-        def _():
-            strips[2].wait_recv()
-            blocks[2].wait_recv()
-            for slot in (7, 8):
-                start(strips, slot)
-                start(blocks, slot)
-
-    relay(jnp.logical_not(crossing))
-    near_part(False, 0, 4)
-    relay(crossing)
-    arrive(blocks, 3)
-    start(blocks, 5)
-    arrive(blocks, 4)
-    start(blocks, 6)
-    for k in near_first:
-        z_arrival(k, 0).wait_recv()
-        z_arrival(k, 1).wait_recv()
-        pass_on(k).start()
-    near_part(False, 4, 12)
-
-    def place_only(slot):
-        row, col = spots[slot]
-        when(routes[slot][1], lambda: place(packed, slot, parents, row, col))
-        if routes[slot][1] is not True:
-
-            @pl.when(jnp.logical_not(routes[slot][1]))
-            def _():
-                for pr in range(3):
-                    for pc in range(2):
-                        parents[row + pr, col + pc] = jnp.zeros(parents.shape[2:], F32)
-
-    for slot in (3, 4, 2):
-        place_only(slot)
-    for slot in (5, 6):
-        settle(slot)
-    for k in range(ZN):
-        pass_on(k).wait_recv()
+    near_side((RIGHT, LEFT))
+    forward(3)
 
     def gather_ops(chunk, carry):
         lanes = pl.ds(pl.multiple_of(chunk * 128, 128), 128)
@@ -403,37 +444,76 @@
         sin_ops[:, lanes] = jnp.where(left, pltpu.roll(even, 64, 1), uneven)
         return carry
 
-    lax.fori_loop(0, 2 * ZN, gather_ops, 0)
     variants = [(a, b) for a in range(2) for b in range(2)]
-    for a, b in variants:
-        pl.when(jnp.logical_and(core == a, odd == b))(
-            lambda a=a, b=b: far_early(parents, cos_ops, sin_ops, on, parent_in, a, b)
+
+    half_pieces = pieces // 2
+
+    def early(i, carry):
+        q = lax.rem(half_pieces * y + i, pieces)
+        for slot in (1, 5, 6):
+            arrive_block(slot, q)
+        for slot in (1, 3, 4, 5, 6):
+            settle(slot, q)
+        lax.fori_loop(q * (PIECE // 128), (q + 1) * (PIECE // 128), gather_ops, 0)
+        for a, b in variants:
+            pl.when(jnp.logical_and(core == a, odd == b))(
+                lambda a=a, b=b: far_early(parents, cos_ops, sin_ops, on, parent_in, a, b, q)
+            )
+        return carry
+
+    for k in range(ZN):
+        pass_on(k, 0).wait_recv()
+    lax.fori_loop(0, half_pieces, early, 0)
+    collect(1)
+    pl.when(crossing)(relay_strips)
+    relay_crossing(*range(pieces))
+    for k in range(ZN):
+        pass_on(k, 1).wait_recv()
+    lax.fori_loop(half_pieces, pieces, early, 0)
+    for slot in (7, 8):
+        arrive(slot)
+    widen(lambda r: outr[r], window, range(10), 6 * core)
+    near_side((LEFT, RIGHT))
+    scale = interp.shape[0] / interp.shape[1]
+
+    def last(q, carry):
+        settle(2, q)
+        for slot in (7, 8):
+            arrive_block(slot, q)
+            settle(slot, q)
+        for a, b in variants:
+            pl.when(jnp.logical_and(core == a, odd == b))(
+                lambda a=a, b=b: far_late(parents, cos_ops, sin_ops, on, parent_in, cosine, sine, child, a, b, q)
+            )
+        lanes = pl.ds(pl.multiple_of(q * PIECE, PIECE), PIECE)
+        back = lax.dot_general(
+            child[:, lanes], interp[:, lanes], (((1,), (1,)), ((), ())), preferred_element_type=F32
         )
-    for slot in (7, 8):
-        arrive(strips, slot)
-    widen(lambda r: outr[r], window, range(10), 6 * core)
-    near_part(True, 0, 12)
-    for slot in (7, 8):
-        settle(slot)
-    for a, b in variants:
-        pl.when(jnp.logical_and(core == a, odd == b))(
-            lambda a=a, b=b: far_late(parents, cos_ops, sin_ops, on, parent_in, cosine, sine, child, a, b)
-        )
-    back = lax.dot_general(child[...], interp[...], (((1,), (1,)), ((), ())), preferred_element_type=F32)
-    scale = interp.shape[0] / interp.shape[1]
+        near[...] += (back * scale).reshape(near.shape)
+        return carry
+
+    lax.fori_loop(0, pieces, last, 0)
     for r in range(6):
         for c in range(4):
-            box = r * 4 + c
-            total = near[box] + back[box * 8 : box * 8 + 8] * scale
+            total = near[r * 4 + c]
             out[r, c, 0] = total[:4]
             out[r, c, 1] = total[4:]
 
-    to_far_done = [z_send(k, half) for k in range(1, ZN) for half in range(2)] + [pass_on(k) for k in range(ZN)]
-    for copy in to_far_done:
+    for copy in [z_send(k, half) for k in range(1, ZN) for half in range(2)] + [
+        pass_on(k, half) for k in range(ZN) for half in range(2)
+    ]:
         copy.wait_send()
-    for kind_of in (strips, blocks):
+    for slot in routes:
+        when(routes[slot][0], lambda slot=slot: strips[slot].wait_send())
+
+    def drain(q, carry):
         for slot in routes:
-            when(routes[slot][0], lambda kind_of=kind_of, slot=slot: kind_of[slot].wait_send())
+            sent_block(slot, q)
+        for slot in (7, 8):
+            pl.when(hand_on[slot])(lambda slot=slot: across(slot, q).wait_send())
+        return carry
+
+    lax.fori_loop(0, pieces, drain, 0)
 
 
 def per_device(
@@ -451,7 +531,7 @@
         in_specs=[hbm] * 7,
         out_specs=pl.BlockSpec(memory_space=pltpu.VMEM),
         scratch_shapes=[
-            vmem((9 * 48, dp), BF16),
+            vmem((dp // PIECE, 9 * 48, PIECE), BF16),
             vmem((10, 2, 16, 512), BF16),
             vmem((10, 16, 512), BF16),
             vmem((10, 16, 512), BF16),
@@ -474,8 +554,8 @@
             vmem((4, dp), F32),
             vmem((kinds, dp), F32),
             vmem((kinds, dp), F32),
-            dma((8,)), dma((8,)), dma((8,)), dma((8,)), dma((8,)), dma((2,)),
-            dma((2, ZN)), dma((2, ZN)), dma((ZN,)), dma((ZN,)),
+            dma((dp // PIECE, 8)), dma((dp // PIECE, 8)), dma((8,)), dma((8,)), dma((8,)), dma((dp // PIECE,)), dma((2,)),
+            dma((2, ZN)), dma((2, ZN)), dma((2, ZN)), dma((2, ZN)),
         ],
         compiler_params=pltpu.CompilerParams(
             collective_id=0, has_side_effects=True, vmem_limit_bytes=56 * 1024 * 1024

time: 39.6 us -> 37.2 us (0.939); the launches traced: 38.9 us -> 36.9 us
  Pallas kernels: 37.1 us -> 35.1 us
    pallas_call x1, Pallas kernels: 37.1 us -> 35.1 us  [per_device(): pl.pallas_call(kernel, out_shape=jax.ShapeDtypeStruct(fine_out.shape, F32...]
where the time goes in v2:
time: 37.2 us; the launch traced here: 36.9 us
  Pallas kernels  35.1 us (94%)
  local copies, waits for them, and re-layouts  1.78 us (5%)
    pallas_call x1, Pallas kernels, per_device(): pl.pallas_call(kernel, out_shape=jax.ShapeDtypeStruct(fine_out.shape, F32...  35.1 us
    unnamed x1, local copies, waits for them, and re-layouts  1.78 us

profile of v2, /device:TPU:56, one launch (start us, length us, event | category | flops | bytes accessed | tf_op | source)
XLA Modules:
  0.0 36.9 jit_solution(18214466208740902711)
XLA Ops:
  0.0 35.1 %fmm.1 = f32[6,4,2,4,512]{4,3,2,1,0:T(4,128)} custom-call(bf16[6,4,2,4,512]{4,3,2,1,0:T(4,128)(2,1)} %x_hbm.1, f32[40,2,64]{2,1,0:T(2,128)} %ops_hbm.1, bf16[512,2048]{1,0:T(8,128)(2,1)} %interp_hbm.1, f32[4,2048]{1,0:T(4,128)} %phase_hbm.1, f32[40,2,512]{2,1,0:T(2,128)} %fine_ops_hbm.1, s32[6,32,128]{2,1,0:T(8,128)} %bitcast.2, s32[3,32,64]{2,1,0:T(8,128)} %bitcast.3), custom_call_target="tpu_custom_call" | custom-call | tf_op jit(solution)/shard_map/fmm/pallas_call | solution.py:528
  35.1 1.8 %copy.9 = f32[6,4,2,4,512]{4,3,2,1,0:T(4,128)} copy(f32[6,4,2,4,512]{4,3,2,1,0:T(4,128)} %fmm.1) | data formatting | bytes 786432

commit v3 on v2

--- a/solution.py
+++ b/solution.py
@@ -65,8 +65,8 @@
 
 def near_field(window, ops, present, near, columns, start, stop):
     def one(step, carry):
-        pair, lane = step // 4, lax.rem(step, 4)
-        lanes = pl.ds(pl.multiple_of(lane * 128, 128), 128)
+        pair, lane = step // 2, lax.rem(step, 2)
+        lanes = pl.ds(pl.multiple_of(lane * 256, 256), 256)
         first, second = {}, {}
         for op, (dr, dc) in enumerate(OFFSETS):
             used = [
@@ -197,8 +197,13 @@
 
     for load in loads[:2]:
         load.start()
-    for q in range(pieces):
-        interp_load(q).start()
+    half_pieces = pieces // 2
+
+    def turn(i, half=y):
+        return lax.rem(half_pieces * half + i, pieces)
+
+    for i in range(pieces):
+        interp_load(turn(i)).start()
     for load in loads[2:]:
         load.start()
     loads[1].wait()
@@ -313,16 +318,21 @@
         ref = opsg.at[core, lax.rem(z - k + ZN, ZN), y if half == 0 else 1 - y]
         return send(ref, ref, es.at[half, k], er.at[half, k], (p, other))
 
-    for slot in (2, 3, 4, 1):
+    patient = d == 2 * ZN
+
+    to_far.start()
+    pl.when(jnp.logical_not(patient))(lambda: start(2))
+    for slot in (3, 4, 1):
         start(slot)
-    to_far.start()
     for k in near_first:
         z_send(k, 0).start()
 
-    def following(q, carry):
+    def following(i, carry):
+        q = turn(i)
         interp_load(q).wait()
         aggregate(own, interp, cosine, sine, packed, parents, q)
-        for slot in (2, 3, 4, 1):
+        pl.when(jnp.logical_not(patient))(lambda: start_block(2, q))
+        for slot in (3, 4, 1):
             start_block(slot, q)
         return carry
 
@@ -396,14 +406,14 @@
     def near_side(columns_of):
         for which in range(2):
             pl.when(core == which)(
-                lambda which=which: near_field(window, fine_ops, on, near, columns_of[which], 0, 12)
+                lambda which=which: near_field(window, fine_ops, on, near, columns_of[which], 0, 6)
             )
 
     def relay_crossing(*qs):
         @pl.when(crossing)
         def _():
-            for q in qs:
-                relay(q)
+            for i in qs:
+                relay(turn(i, 1 - y))
 
     def collect(half):
         for k in near_first:
@@ -417,24 +427,31 @@
         widen(lambda r, c=c: own[r, c], window, range(10), 2 + 2 * c)
     to_smem.wait()
     loads[5].wait()
-    near_field(window, fine_ops, on, near, OWN, 0, 4)
+    near_field(window, fine_ops, on, near, OWN, 0, 2)
     to_far.wait()
     for k in near_first:
         z_send(k, 1).start()
     for half in range(2):
         pass_on(0, half).start()
-    forward(0)
-    near_field(window, fine_ops, on, near, OWN, 4, 8)
-    forward(1)
+    forward(turn(0))
+    near_field(window, fine_ops, on, near, OWN, 2, 4)
+
+    @pl.when(patient)
+    def _():
+        start(2)
+        for i in range(pieces):
+            start_block(2, turn(i))
+
+    forward(turn(1))
     pl.when(direct)(relay_strips)
-    near_field(window, fine_ops, on, near, OWN, 8, 12)
+    near_field(window, fine_ops, on, near, OWN, 4, 6)
     collect(0)
-    forward(2)
+    forward(turn(2))
     for slot in (1, 5, 6):
         arrive(slot)
     widen(lambda r: oth[r], window, range(10), 6 - 6 * core)
     near_side((RIGHT, LEFT))
-    forward(3)
+    forward(turn(3))
 
     def gather_ops(chunk, carry):
         lanes = pl.ds(pl.multiple_of(chunk * 128, 128), 128)
@@ -446,10 +463,8 @@
 
     variants = [(a, b) for a in range(2) for b in range(2)]
 
-    half_pieces = pieces // 2
-
     def early(i, carry):
-        q = lax.rem(half_pieces * y + i, pieces)
+        q = turn(i)
         for slot in (1, 5, 6):
             arrive_block(slot, q)
         for slot in (1, 3, 4, 5, 6):
@@ -465,18 +480,25 @@
         pass_on(k, 0).wait_recv()
     lax.fori_loop(0, half_pieces, early, 0)
     collect(1)
+
+    def second_half():
+        for k in range(ZN):
+            pass_on(k, 1).wait_recv()
+        lax.fori_loop(half_pieces, pieces, early, 0)
+
     pl.when(crossing)(relay_strips)
     relay_crossing(*range(pieces))
-    for k in range(ZN):
-        pass_on(k, 1).wait_recv()
-    lax.fori_loop(half_pieces, pieces, early, 0)
+    pl.when(crossing)(second_half)
     for slot in (7, 8):
         arrive(slot)
     widen(lambda r: outr[r], window, range(10), 6 * core)
     near_side((LEFT, RIGHT))
     scale = interp.shape[0] / interp.shape[1]
 
-    def last(q, carry):
+    order = jnp.where(crossing, 1 - y, y)
+
+    def last(i, carry):
+        q = turn(i, order)
         settle(2, q)
         for slot in (7, 8):
             arrive_block(slot, q)
@@ -492,7 +514,9 @@
         near[...] += (back * scale).reshape(near.shape)
         return carry
 
-    lax.fori_loop(0, pieces, last, 0)
+    lax.fori_loop(0, half_pieces, last, 0)
+    pl.when(jnp.logical_not(crossing))(second_half)
+    lax.fori_loop(half_pieces, pieces, last, 0)
     for r in range(6):
         for c in range(4):
             total = near[r * 4 + c]

time: 37.2 us -> 37 us (level)
  no operation moved by 1% of the time
where the time goes in v3:
time: 37 us; the launch traced here: 36.9 us
  Pallas kernels  35.1 us (95%)
  local copies, waits for them, and re-layouts  1.78 us (5%)
    pallas_call x1, Pallas kernels, per_device(): pl.pallas_call(kernel, out_shape=jax.ShapeDtypeStruct(fine_out.shape, F32...  35.1 us
    unnamed x1, local copies, waits for them, and re-layouts  1.78 us

profile of v3, /device:TPU:56, one launch (start us, length us, event | category | flops | bytes accessed | tf_op | source)
XLA Modules:
  0.0 36.9 jit_solution(7089844675734175076)
XLA Ops:
  0.0 35.1 %fmm.1 = f32[6,4,2,4,512]{4,3,2,1,0:T(4,128)} custom-call(bf16[6,4,2,4,512]{4,3,2,1,0:T(4,128)(2,1)} %x_hbm.1, f32[40,2,64]{2,1,0:T(2,128)} %ops_hbm.1, bf16[512,2048]{1,0:T(8,128)(2,1)} %interp_hbm.1, f32[4,2048]{1,0:T(4,128)} %phase_hbm.1, f32[40,2,512]{2,1,0:T(2,128)} %fine_ops_hbm.1, s32[6,32,128]{2,1,0:T(8,128)} %bitcast.2, s32[3,32,64]{2,1,0:T(8,128)} %bitcast.3), custom_call_target="tpu_custom_call" | custom-call | tf_op jit(solution)/shard_map/fmm/pallas_call | solution.py:552
  35.1 1.8 %copy.9 = f32[6,4,2,4,512]{4,3,2,1,0:T(4,128)} copy(f32[6,4,2,4,512]{4,3,2,1,0:T(4,128)} %fmm.1) | data formatting | bytes 786432
